TPU v7x, 32 devices: a whole 2x2x4 slice. The times are simulated.
32 devices in a mesh: dp: 16 (over z, y, x), fsdp: 2 (over core).
Axes of the slice: x: 2, y: 2, z: 4, core: 2. Of those that a mesh axis runs over, the one named last changes fastest.
Arguments:
- tokens: bfloat16 [2, 18432, 1024], P(None, ('dp', 'fsdp')), may hold values from -6 to 6
- cotangent: bfloat16 [2, 18432, 1024], P(None, ('dp', 'fsdp')), may hold values from -6 to 6
- images: int32 [2, 16, 3], P(None, 'dp'), may hold values from 0 to 4, as said below
- attention_weight: float32 [4096, 1024], P(('dp', 'fsdp')), may hold values from -1 to 1
- attention_first: float32 [4096, 1024], P(('dp', 'fsdp')), may hold values from -0.00048828125 to 0.00048828125
- attention_second: float32 [4096, 1024], P(('dp', 'fsdp')), may hold values from 7.7838555e-11 to 3.1135422e-10
- widen_weight: float32 [1024, 5632], P(None, ('dp', 'fsdp')), may hold values from -0.1875 to 0.1875
- widen_first: float32 [1024, 5632], P(None, ('dp', 'fsdp')), may hold values from -0.00048828125 to 0.00048828125
- widen_second: float32 [1024, 5632], P(None, ('dp', 'fsdp')), may hold values from 7.7838555e-11 to 3.1135422e-10
- narrow_weight: float32 [2816, 1024], P(('dp', 'fsdp')), may hold values from -0.109375 to 0.109375
- narrow_first: float32 [2816, 1024], P(('dp', 'fsdp')), may hold values from -0.00048828125 to 0.00048828125
- narrow_second: float32 [2816, 1024], P(('dp', 'fsdp')), may hold values from 7.7838555e-11 to 3.1135422e-10
- norm_gains: float32 [2048], P(('dp', 'fsdp')), may hold values from 0.5 to 1.5
- gains_first: float32 [2048], P(('dp', 'fsdp')), may hold values from -0.0014648438 to 0.0014648438
- gains_second: float32 [2048], P(('dp', 'fsdp')), may hold values from 7.00547e-10 to 2.802188e-09
Outputs:
- block_output: float32 [2, 18432, 1024], P(None, ('dp', 'fsdp'))
- input_grad: float32 [2, 18432, 1024], P(None, ('dp', 'fsdp'))
- attention_master: float32 [4096, 1024], P(('dp', 'fsdp'))
- attention_mean: float32 [4096, 1024], P(('dp', 'fsdp'))
- attention_square: float32 [4096, 1024], P(('dp', 'fsdp'))
- widen_master: float32 [1024, 5632], P(None, ('dp', 'fsdp'))
- widen_mean: float32 [1024, 5632], P(None, ('dp', 'fsdp'))
- widen_square: float32 [1024, 5632], P(None, ('dp', 'fsdp'))
- narrow_master: float32 [2816, 1024], P(('dp', 'fsdp'))
- narrow_mean: float32 [2816, 1024], P(('dp', 'fsdp'))
- narrow_square: float32 [2816, 1024], P(('dp', 'fsdp'))
- gains_master: float32 [2048], P(('dp', 'fsdp'))
- gains_mean: float32 [2048], P(('dp', 'fsdp'))
- gains_square: float32 [2048], P(('dp', 'fsdp'))
- grad_norm: float32 [], replicated
Inputs may be any that keep to these rules, and one draw needn't show every extreme that they name: Each packed row's 3 slots are one of (4, 0, 0), (1, 1, 1), (2, 1, 0), (1, 2, 0): the images of the row's items in order, a 0 marking an empty slot.
All inputs are finite; a program needn't handle non-finite values.
Results may differ from a plain program's by a relative error of at most 0.014.
The roundings to bfloat16 on the way count: a program that leaves them out, or rounds other values in their place, can miss the bound.
Values may be sent and summed in bfloat16 or wider, within the bound.
A program may use at most 320 MiB of HBM per device.

v0:
```python
import jax
import jax.numpy as jnp
from jax import lax
from jax.sharding import PartitionSpec as P

HD = 64
TEXT = 128
PATCH = 256
ROW = 1152
NORM_EPS = 1e-06
MASKED = -1000000000.0
BETA_FIRST = 0.9
BETA_SECOND = 0.999
ADAM_EPS = 1e-08
MATRIX_RATE = 0.05
GAIN_RATE = 0.3
DECAY = 0.1
CLIP_LIMIT = 1.0
STEP_VALUE = 10.0


def gelu_tanh(values):
    return (
        0.5
        * values
        * (1.0 + jnp.tanh(0.7978845608028654 * (values + 0.044715 * values * values * values)))
    )


def gated_units(gate_pre, upward):
    return gelu_tanh(gate_pre) * upward


def rms_scale(values, gain_vector):
    return (
        values
        * lax.rsqrt(jnp.mean(values * values, axis=-1, keepdims=True) + NORM_EPS)
        * gain_vector
    )


def segment_ids(counts):
    item_sizes = jnp.where(counts > 0, TEXT + PATCH * counts, 0)
    item_ends = jnp.cumsum(item_sizes)
    places = jnp.arange(ROW, dtype=jnp.int32)
    return jnp.sum((places[:, None] >= item_ends[None, :]).astype(jnp.int32), axis=1)


def contract_rows(left, right):
    return lax.dot_general(
        left, right, (((0,), (0,)), ((), ())), preferred_element_type=jnp.float32
    )


def contract_cols(left, right):
    return lax.dot_general(
        left, right, (((1,), (1,)), ((), ())), preferred_element_type=jnp.float32
    )


def head_pairs(values):
    return values.reshape(values.shape[0], values.shape[1] // (2 * HD), 2 * HD).transpose(1, 0, 2)


def from_pairs(values):
    return values.transpose(1, 0, 2).reshape(values.shape[1], values.shape[0] * values.shape[2])


def flat_grads(grads):
    return (
        grads[0].reshape(-1, 128),
        grads[1].reshape(-1, 128),
        grads[2].reshape(-1, 128),
        grads[3],
    )


def shard_grads(reduced, model_width):
    widen_part = reduced[1].reshape(-1, model_width).T
    return (
        reduced[0].reshape(-1, model_width),
        widen_part,
        reduced[2].reshape(-1, model_width),
        reduced[3],
    )


def pair_forward(query_rows, key_rows, value_rows, same_item):
    query_heads = query_rows.reshape(query_rows.shape[0], 2, HD)
    key_heads = key_rows.reshape(key_rows.shape[0], 2, HD)
    value_heads = value_rows.reshape(value_rows.shape[0], 2, HD)
    scores = jnp.einsum("shd,khd->hsk", query_heads, key_heads, preferred_element_type=jnp.float32)
    scores = jnp.where(same_item[None], scores, MASKED)
    row_top = jnp.max(scores, axis=-1, keepdims=True)
    shifted = jnp.exp(scores - row_top)
    row_total = jnp.sum(shifted, axis=-1, keepdims=True)
    attend = shifted / row_total
    log_total = (row_top + jnp.log(row_total))[..., 0]
    mixed_heads = jnp.einsum(
        "hsk,khd->shd", attend.astype(jnp.bfloat16), value_heads, preferred_element_type=jnp.float32
    )
    return (mixed_heads.reshape(query_rows.shape[0], 2 * HD), log_total)


def pair_backward(query_rows, key_rows, value_rows, grad_rows, log_total, same_item):
    query_heads = query_rows.reshape(query_rows.shape[0], 2, HD)
    key_heads = key_rows.reshape(key_rows.shape[0], 2, HD)
    value_heads = value_rows.reshape(value_rows.shape[0], 2, HD)
    grad_heads = grad_rows.reshape(grad_rows.shape[0], 2, HD)
    scores = jnp.einsum("shd,khd->hsk", query_heads, key_heads, preferred_element_type=jnp.float32)
    scores = jnp.where(same_item[None], scores, MASKED)
    attend = jnp.exp(scores - log_total[..., None])
    grad_attend = jnp.einsum(
        "shd,khd->hsk", grad_heads, value_heads, preferred_element_type=jnp.float32
    )
    inner_sum = jnp.sum(attend * grad_attend, axis=-1, keepdims=True)
    grad_scores = (attend * (grad_attend - inner_sum)).astype(jnp.bfloat16)
    grad_query = jnp.einsum(
        "hsk,khd->shd", grad_scores, key_heads, preferred_element_type=jnp.float32
    )
    grad_key = jnp.einsum(
        "hsk,shd->khd", grad_scores, query_heads, preferred_element_type=jnp.float32
    )
    grad_value = jnp.einsum(
        "hsk,shd->khd", attend.astype(jnp.bfloat16), grad_heads, preferred_element_type=jnp.float32
    )
    query_count = query_rows.shape[0]
    key_count = key_rows.shape[0]
    return (
        grad_query.reshape(query_count, 2 * HD),
        grad_key.reshape(key_count, 2 * HD),
        grad_value.reshape(key_count, 2 * HD),
    )


def adam_update(master, first, second, gradient, factors, rate, decay):
    clip_factor, first_fix, second_fix = factors
    clipped = clip_factor * gradient
    first_new = BETA_FIRST * first + (1.0 - BETA_FIRST) * clipped
    second_new = BETA_SECOND * second + (1.0 - BETA_SECOND) * clipped * clipped
    master_new = master - rate * (
        first_new / first_fix / (jnp.sqrt(second_new / second_fix) + ADAM_EPS) + decay * master
    )
    return (master_new, first_new, second_new)


def local(
    tokens,
    cotangent,
    images,
    attention_weight,
    attention_first,
    attention_second,
    widen_weight,
    widen_first,
    widen_second,
    narrow_weight,
    narrow_first,
    narrow_second,
    norm_gains,
    gains_first,
    gains_second,
):
    model_width = tokens.shape[2]
    row_count = tokens.shape[1]
    hidden_width = narrow_weight.shape[0] * lax.axis_size(("dp", "fsdp"))
    half_index = lax.axis_index("fsdp")
    attention_low = attention_weight.astype(jnp.bfloat16)
    widen_low = widen_weight.astype(jnp.bfloat16)
    narrow_low = narrow_weight.astype(jnp.bfloat16)
    gains_low = norm_gains.astype(jnp.bfloat16)

    def forward(full_weights, rows_in, same_item):
        attention_full, widen_full, narrow_full, gains_full = full_weights
        matrices = attention_full.reshape(4, model_width, model_width)
        first_gain = gains_full[:model_width].astype(jnp.float32)
        second_gain = gains_full[model_width:].astype(jnp.float32)
        inputs = rows_in.astype(jnp.float32)
        normed = rms_scale(inputs, first_gain).astype(jnp.bfloat16)
        projected = jnp.einsum(
            "sd,jde->jse", normed, matrices[:3], preferred_element_type=jnp.float32
        ).astype(jnp.bfloat16)
        keys_all, values_all = (
            lax.all_gather(projected[1], "fsdp", axis=0, tiled=True),
            lax.all_gather(projected[2], "fsdp", axis=0, tiled=True),
        )
        mixed_heads, log_total = lax.map(
            lambda pieces: pair_forward(pieces[0], pieces[1], pieces[2], same_item),
            (head_pairs(projected[0]), head_pairs(keys_all), head_pairs(values_all)),
        )
        mixed_heads = from_pairs(mixed_heads).astype(jnp.bfloat16)
        hidden_one = inputs + jnp.dot(mixed_heads, matrices[3], preferred_element_type=jnp.float32)
        second = rms_scale(hidden_one, second_gain).astype(jnp.bfloat16)
        widened = jnp.dot(second, widen_full, preferred_element_type=jnp.float32)
        gate_pre = widened[:, :hidden_width]
        upward = widened[:, hidden_width:]
        hidden = gated_units(gate_pre, upward).astype(jnp.bfloat16)
        result = hidden_one + jnp.dot(hidden, narrow_full, preferred_element_type=jnp.float32)
        saved = (
            inputs,
            normed,
            projected[0],
            keys_all,
            values_all,
            log_total,
            mixed_heads,
            hidden_one,
            second,
            gate_pre,
            upward,
            hidden,
        )
        return (result, saved)

    def backward(full_weights, saved, grad_rows, same_item):
        attention_full, widen_full, narrow_full, gains_full = full_weights
        matrices = attention_full.reshape(4, model_width, model_width)
        first_gain = gains_full[:model_width].astype(jnp.float32)
        second_gain = gains_full[model_width:].astype(jnp.float32)
        (
            inputs,
            normed,
            query_rows,
            keys_all,
            values_all,
            log_total,
            mixed_heads,
            hidden_one,
            second,
            gate_pre,
            upward,
            hidden,
        ) = saved
        grad_narrow = contract_rows(hidden, grad_rows)
        grad_hidden = contract_cols(grad_rows, narrow_full)
        unused_value, gated_back = jax.vjp(gated_units, gate_pre, upward)
        grad_gate, grad_up = gated_back(grad_hidden)
        grad_widened = jnp.concatenate([grad_gate, grad_up], axis=1).astype(jnp.bfloat16)
        grad_widen_cols = contract_rows(grad_widened, second)
        grad_second = contract_cols(grad_widened, widen_full)
        unused_norm, second_back = jax.vjp(rms_scale, hidden_one, second_gain)
        grad_from_norm, grad_gain_two = second_back(grad_second)
        grad_hidden_one = grad_rows.astype(jnp.float32) + grad_from_norm
        grad_branch = grad_hidden_one.astype(jnp.bfloat16)
        grad_output_proj = contract_rows(mixed_heads, grad_branch)
        grad_mixed = contract_cols(grad_branch, matrices[3]).astype(jnp.bfloat16)
        grad_query, grad_key, grad_value = lax.map(
            lambda pieces: pair_backward(
                pieces[0], pieces[1], pieces[2], pieces[3], pieces[4], same_item
            ),
            (
                head_pairs(query_rows),
                head_pairs(keys_all),
                head_pairs(values_all),
                head_pairs(grad_mixed),
                log_total,
            ),
        )
        own_key, own_value = (
            lax.psum_scatter(
                from_pairs(grad_key).astype(jnp.bfloat16), "fsdp", scatter_dimension=0, tiled=True
            ).astype(jnp.float32),
            lax.psum_scatter(
                from_pairs(grad_value).astype(jnp.bfloat16), "fsdp", scatter_dimension=0, tiled=True
            ).astype(jnp.float32),
        )
        grad_projected = jnp.stack([from_pairs(grad_query), own_key, own_value]).astype(
            jnp.bfloat16
        )
        grad_qkv = jnp.einsum(
            "sd,jse->jde", normed, grad_projected, preferred_element_type=jnp.float32
        )
        grad_normed = jnp.einsum(
            "jse,jde->sd", grad_projected, matrices[:3], preferred_element_type=jnp.float32
        )
        unused_first, first_back = jax.vjp(rms_scale, inputs, first_gain)
        grad_from_first, grad_gain_one = first_back(grad_normed)
        input_rows = grad_hidden_one + grad_from_first
        grad_attention = jnp.concatenate([grad_qkv, grad_output_proj[None]], axis=0).reshape(
            4 * model_width, model_width
        )
        grad_gains = jnp.concatenate([grad_gain_one, grad_gain_two])
        return (input_rows, (grad_attention, grad_widen_cols, grad_narrow, grad_gains))

    start_grads = (
        jnp.zeros((4 * model_width, model_width), jnp.float32),
        jnp.zeros((2 * hidden_width, model_width), jnp.float32),
        jnp.zeros((hidden_width, model_width), jnp.float32),
        jnp.zeros((2 * model_width,), jnp.float32),
    )

    def micro_step(running, pieces):
        rows_in, grad_rows, counts = pieces
        seg_full = segment_ids(counts)
        seg_own = lax.dynamic_slice_in_dim(seg_full, half_index * row_count, row_count)
        same_item = seg_own[:, None] == seg_full[None, :]
        forward_weights = (
            lax.all_gather(attention_low, ("dp", "fsdp"), axis=0, tiled=True),
            lax.all_gather(widen_low, ("dp", "fsdp"), axis=1, tiled=True),
            lax.all_gather(narrow_low, ("dp", "fsdp"), axis=0, tiled=True),
            lax.all_gather(gains_low, ("dp", "fsdp"), axis=0, tiled=True),
        )
        result, saved = forward(forward_weights, rows_in, same_item)
        backward_weights = (
            lax.all_gather(attention_low, ("dp", "fsdp"), axis=0, tiled=True),
            lax.all_gather(widen_low, ("dp", "fsdp"), axis=1, tiled=True),
            lax.all_gather(narrow_low, ("dp", "fsdp"), axis=0, tiled=True),
            lax.all_gather(gains_low, ("dp", "fsdp"), axis=0, tiled=True),
        )
        input_rows, gradients = backward(backward_weights, saved, grad_rows, same_item)
        running = tuple((total + fresh for total, fresh in zip(running, gradients)))
        return (running, (result, input_rows))

    totals, (block_output, input_grad) = lax.scan(
        micro_step, start_grads, (tokens, cotangent, images[:, 0, :])
    )
    flat_list = flat_grads(totals)
    summed = (
        lax.psum_scatter(flat_list[0], ("dp", "fsdp"), scatter_dimension=0, tiled=True),
        lax.psum_scatter(flat_list[1], ("dp", "fsdp"), scatter_dimension=0, tiled=True),
        lax.psum_scatter(flat_list[2], ("dp", "fsdp"), scatter_dimension=0, tiled=True),
        lax.psum_scatter(flat_list[3], ("dp", "fsdp"), scatter_dimension=0, tiled=True),
    )
    reduced = shard_grads(summed, model_width)
    local_squares = (
        jnp.sum(reduced[0] * reduced[0])
        + jnp.sum(reduced[1] * reduced[1])
        + jnp.sum(reduced[2] * reduced[2])
        + jnp.sum(reduced[3] * reduced[3])
    )
    grad_norm = jnp.sqrt(lax.psum(local_squares, ("dp", "fsdp")))
    clip_factor = jnp.minimum(1.0, CLIP_LIMIT / (grad_norm + 1e-06))
    step_value = jnp.float32(STEP_VALUE)
    factors = (
        clip_factor,
        1.0 - jnp.power(jnp.float32(BETA_FIRST), step_value),
        1.0 - jnp.power(jnp.float32(BETA_SECOND), step_value),
    )
    attention_master, attention_mean, attention_square = adam_update(
        attention_weight, attention_first, attention_second, reduced[0], factors, MATRIX_RATE, DECAY
    )
    widen_master, widen_mean, widen_square = adam_update(
        widen_weight, widen_first, widen_second, reduced[1], factors, MATRIX_RATE, DECAY
    )
    narrow_master, narrow_mean, narrow_square = adam_update(
        narrow_weight, narrow_first, narrow_second, reduced[2], factors, MATRIX_RATE, DECAY
    )
    gains_master, gains_mean, gains_square = adam_update(
        norm_gains, gains_first, gains_second, reduced[3], factors, GAIN_RATE, 0.0
    )
    return (
        block_output,
        input_grad,
        attention_master,
        attention_mean,
        attention_square,
        widen_master,
        widen_mean,
        widen_square,
        narrow_master,
        narrow_mean,
        narrow_square,
        gains_master,
        gains_mean,
        gains_square,
        grad_norm,
    )


def solution(mesh):
    placed = (
        P(None, ("dp", "fsdp"), None),
        P(None, ("dp", "fsdp"), None),
        P(None, "dp", None),
        P(("dp", "fsdp"), None),
        P(("dp", "fsdp"), None),
        P(("dp", "fsdp"), None),
        P(None, ("dp", "fsdp")),
        P(None, ("dp", "fsdp")),
        P(None, ("dp", "fsdp")),
        P(("dp", "fsdp"), None),
        P(("dp", "fsdp"), None),
        P(("dp", "fsdp"), None),
        P(("dp", "fsdp")),
        P(("dp", "fsdp")),
        P(("dp", "fsdp")),
    )
    return jax.shard_map(
        local,
        mesh=mesh,
        in_specs=placed,
        out_specs=(
            P(None, ("dp", "fsdp"), None),
            P(None, ("dp", "fsdp"), None),
            P(("dp", "fsdp"), None),
            P(("dp", "fsdp"), None),
            P(("dp", "fsdp"), None),
            P(None, ("dp", "fsdp")),
            P(None, ("dp", "fsdp")),
            P(None, ("dp", "fsdp")),
            P(("dp", "fsdp"), None),
            P(("dp", "fsdp"), None),
            P(("dp", "fsdp"), None),
            P(("dp", "fsdp")),
            P(("dp", "fsdp")),
            P(("dp", "fsdp")),
            P(),
        ),
        check_vma=False,
    )
```

profile of v0, /device:TPU:0, one launch (start us, length us, event | category | flops | bytes accessed | tf_op | source)
XLA Modules:
  0.0 1677.6 jit_solution(11807096123481081183)
XLA Ops:
  12.5 999.1 %while.73 = (s32[]{:T(128)}, f32[4096,1024]{1,0:T(8,128)}, f32[5632,1024]{1,0:T(8,128)}, f32[2816,1024]{1,0:T(8,128)}, f32[2048]{0:T(1024)}, /*index=5*/f32[2,57...) while((s32[]{:T(128)}, f32[4096,1024]{1,0:T(8,128)}, ...), condition=%wide.region_18.19_spmd.clone, body=%wide.region_0.18_spmd.clone.sunk | while | flops 45746876416 | bytes 740799360 | solution.py:314
  14.2 42.5 %all-reduce.4 = bf16[2048]{0:T(1024)(128)(2,1)S(1)} all-reduce(bf16[2048]{0:T(1024)(128)(2,1)S(1)} %dynamic-update-slice.3), channel_id=1, replica_groups=mesh['dp'=16,'fsdp'=2] {'dp','fsdp'}, use_global_device_ids=true, to_apply=%add | all-reduce | flops 2048 | bytes 8192 | tf_op jit(solution)/shard_map/while
  58.4 39.4 %all-gather.14.cloned.1.call-done = bf16[4096,1024]{1,0:T(8,128)(2,1)} async-done(((bf16[128,1024]{1,0:T(8,128)(2,1)}), bf16[4096,1024]{1,0:T(8,128)(2,1)}) %all-gather.14.cloned.1.call-update) | async-done | bytes 8388624 | tf_op jit(solution)/shard_map/while/body/eval_jaxpr/all_gather | solution.py:298
  120.1 10.7 all-gather.18.cloned.1.call-done
  136.3 59.2 %while.74 = (s32[]{:T(128)}, bf16[8,576,128]{1,2,0:T(8,128)(2,1)}, f32[8,2,576]{2,1,0:T(2,128)}, bf16[8,1152,128]{1,2,0:T(8,128)(2,1)S(1)}, bf16[8,576,128]{1,2,...) while((s32[]{:T(128)}, bf16[8,576,128]{1,2,0:T(8,128)(2,1)}, ...), condition=%wide.region_7.7_spmd.clone, body=%wide.region_4.6_spmd.clone.sunk | while | flops 349690752 | bytes 19968356 | solution.py:187
  200.8 25.7 %all-gather.20.cloned.1.call-done = bf16[1024,5632]{0,1:T(8,128)(2,1)} async-done(((bf16[1024,176]{0,1:T(8,128)(2,1)}), bf16[1024,5632]{0,1:T(8,128)(2,1)}) %all-gather.20.cloned.1.call-update) | async-done | bytes 11534352 | tf_op jit(solution)/shard_map/while/body/eval_jaxpr/all_gather | solution.py:299
  226.5 13.3 fusion.176
  239.8 55.6 %all-gather.22.cloned.1.call-done = bf16[2816,1024]{1,0:T(8,128)(2,1)} async-done(((bf16[88,1024]{1,0:T(8,128)(2,1)}), bf16[2816,1024]{1,0:T(8,128)(2,1)}) %all-gather.22.cloned.1.call-update) | async-done | bytes 5767184 | tf_op jit(solution)/shard_map/while/body/eval_jaxpr/all_gather | solution.py:307
  295.4 16.1 fusion.177
  311.5 13.0 multiply_reduce_fusion.12
  332.4 90.6 %while.75 = (s32[]{:T(128)}, bf16[8,576,128]{1,2,0:T(8,128)(2,1)}, bf16[8,1152,128]{1,2,0:T(8,128)(2,1)}, bf16[8,1152,128]{1,2,0:T(8,128)(2,1)}, bf16[8,1152,128...) while((s32[]{:T(128)}, bf16[8,576,128]{1,2,0:T(8,128)(2,1)}, ...), condition=%wide.region_12.12_spmd.clone, body=%wide.region_10.11_spmd.clone.sunk | while | flops 860625792 | bytes 46643592 | solution.py:247
  456.1 16.1 select_add_fusion.4
  492.2 10.9 bitcast_add_fusion.2
  507.7 40.3 %all-reduce.4 = bf16[2048]{0:T(1024)(128)(2,1)S(1)} all-reduce(bf16[2048]{0:T(1024)(128)(2,1)S(1)} %dynamic-update-slice.3), channel_id=1, replica_groups=mesh['dp'=16,'fsdp'=2] {'dp','fsdp'}, use_global_device_ids=true, to_apply=%add | all-reduce | flops 2048 | bytes 8192 | tf_op jit(solution)/shard_map/while
  549.7 38.0 %all-gather.14.cloned.1.call-done = bf16[4096,1024]{1,0:T(8,128)(2,1)} async-done(((bf16[128,1024]{1,0:T(8,128)(2,1)}), bf16[4096,1024]{1,0:T(8,128)(2,1)}) %all-gather.14.cloned.1.call-update) | async-done | bytes 8388624 | tf_op jit(solution)/shard_map/while/body/eval_jaxpr/all_gather | solution.py:298
  626.0 59.2 %while.74 = (s32[]{:T(128)}, bf16[8,576,128]{1,2,0:T(8,128)(2,1)}, f32[8,2,576]{2,1,0:T(2,128)}, bf16[8,1152,128]{1,2,0:T(8,128)(2,1)S(1)}, bf16[8,576,128]{1,2,...) while((s32[]{:T(128)}, bf16[8,576,128]{1,2,0:T(8,128)(2,1)}, ...), condition=%wide.region_7.7_spmd.clone, body=%wide.region_4.6_spmd.clone.sunk | while | flops 349690752 | bytes 19968356 | solution.py:187
  690.5 25.9 %all-gather.20.cloned.1.call-done = bf16[1024,5632]{0,1:T(8,128)(2,1)} async-done(((bf16[1024,176]{0,1:T(8,128)(2,1)}), bf16[1024,5632]{0,1:T(8,128)(2,1)}) %all-gather.20.cloned.1.call-update) | async-done | bytes 11534352 | tf_op jit(solution)/shard_map/while/body/eval_jaxpr/all_gather | solution.py:299
  716.4 13.3 fusion.176
  729.7 55.6 %all-gather.22.cloned.1.call-done = bf16[2816,1024]{1,0:T(8,128)(2,1)} async-done(((bf16[88,1024]{1,0:T(8,128)(2,1)}), bf16[2816,1024]{1,0:T(8,128)(2,1)}) %all-gather.22.cloned.1.call-update) | async-done | bytes 5767184 | tf_op jit(solution)/shard_map/while/body/eval_jaxpr/all_gather | solution.py:307
  785.2 16.4 fusion.177
  801.7 13.0 multiply_reduce_fusion.12
  822.6 90.5 %while.75 = (s32[]{:T(128)}, bf16[8,576,128]{1,2,0:T(8,128)(2,1)}, bf16[8,1152,128]{1,2,0:T(8,128)(2,1)}, bf16[8,1152,128]{1,2,0:T(8,128)(2,1)}, bf16[8,1152,128...) while((s32[]{:T(128)}, bf16[8,576,128]{1,2,0:T(8,128)(2,1)}, ...), condition=%wide.region_12.12_spmd.clone, body=%wide.region_10.11_spmd.clone.sunk | while | flops 860625792 | bytes 46643592 | solution.py:247
  948.8 22.0 %select_add_fusion.4 = f32[5632,1024]{1,0:T(8,128)} fusion(f32[5632,1024]{1,0:T(8,128)} %get-tuple-element.887, pred[]{:T(512)S(6)} %compare.3, bf16[576,2816]{1,0:T(8,128)(2,1)} %copy-done.44, bf16[576,2816]{1,0:T(8,128)(2,1)} %copy-done.43, f32[576,1024]{1,0:T(8,128)S(1)} %copy-done.6, f32[1024]{0:T(1024)S(1)} %get-tuple-element.758, ...), kind=kOutput, calls=%fused_computation.27.clone.1 | convolution fusion | flops 6670057472 | bytes 54991104 | tf_op jit(solution)/shard_map/while/body/eval_jaxpr/dot_general | solution.py:50
  990.8 14.0 bitcast_add_fusion.2
  1011.6 13.3 reshape.263
  1025.0 18.1 %reshape.261 = f32[32768,128]{1,0:T(8,128)} reshape(f32[4096,1024]{1,0:T(8,128)} %get-tuple-element.288) | data formatting | bytes 33554432 | tf_op jit(solution)/shard_map/reshape | solution.py:71
  1043.1 24.6 %reshape.262 = f32[45056,128]{1,0:T(8,128)} reshape(f32[5632,1024]{1,0:T(8,128)} %get-tuple-element.289) | data formatting | bytes 46137344 | tf_op jit(solution)/shard_map/reshape | solution.py:72
  1068.5 42.4 %all-reduce.2 = f32[2048]{0:T(1024)S(1)} all-reduce(f32[2048]{0:T(1024)S(1)} %copy-done.34), channel_id=9, replica_groups=mesh['dp'=16,'fsdp'=2] {'dp','fsdp'}, use_global_device_ids=true, to_apply=%region_25.26.clone | all-reduce | flops 2048 | bytes 16384
  1111.5 67.6 %reduce-scatter.10.cloned.1.call-done = f32[704,128]{1,0:T(8,128)} async-done(((f32[22528,128]{1,0:T(8,128)}), f32[704,128]{1,0:T(8,128)}) %reduce-scatter.10.cloned.1.call-update) | async-done | bytes 360464 | tf_op jit(solution)/shard_map/reduce_scatter | solution.py:321
  1180.7 179.4 %reduce-scatter.6.cloned.1.call-done = f32[1024,128]{1,0:T(8,128)} async-done(((f32[32768,128]{1,0:T(8,128)}), f32[1024,128]{1,0:T(8,128)}) %reduce-scatter.6.cloned.1.call-update) | async-done | bytes 524304 | tf_op jit(solution)/shard_map/reduce_scatter | solution.py:319
  1361.9 248.2 %reduce-scatter.8.cloned.1.call-done = f32[1408,128]{1,0:T(8,128)} async-done(((f32[45056,128]{1,0:T(8,128)}), f32[1408,128]{1,0:T(8,128)}) %reduce-scatter.8.cloned.1.call-update) | async-done | bytes 720912 | tf_op jit(solution)/shard_map/reduce_scatter | solution.py:320
  1614.7 44.6 %psum.7 = f32[]{:T(128)} all-reduce(f32[]{:T(128)S(6)} %add.212), channel_id=1, replica_groups=mesh['dp'=16,'fsdp'=2] {'dp','fsdp'}, use_global_device_ids=true, to_apply=%region_27.28 | all-reduce | flops 1 | bytes 8 | tf_op jit(solution)/shard_map/psum | solution.py:331
  (649 shorter events, 530.1 us)
Async XLA Ops:
  12.5 88.7 %copy-start.10 = (bf16[1024,176]{0,1:T(8,128)(2,1)}, bf16[1024,176]{0,1:T(8,128)(2,1)S(1)}, u32[]{:S(2)}) copy-start(bf16[1024,176]{0,1:T(8,128)(2,1)S(1)} %get-tuple-element.921) | copy-start | bytes 1081348 | tf_op jit(solution)/shard_map/while
  12.5 88.7 %copy-start.14 = (bf16[88,1024]{1,0:T(8,128)(2,1)}, bf16[88,1024]{1,0:T(8,128)(2,1)S(1)}, u32[]{:S(2)}) copy-start(bf16[88,1024]{1,0:T(8,128)(2,1)S(1)} %get-tuple-element.922) | copy-start | bytes 540676 | tf_op jit(solution)/shard_map/while
  12.5 85.2 %all-gather.14.cloned.1.call-start = ((), (), s32[]{:S(2)}) async-start(), calls=%async_computation.8 | async-start | bytes 8650752 | tf_op jit(solution)/shard_map/while/body/eval_jaxpr/all_gather | solution.py:298
  13.3 103.9 %all-gather.16.cloned.1.call-start = ((), (), s32[]{:S(2)}) async-start(), calls=%async_computation.9 | async-start | bytes 3538944 | tf_op jit(solution)/shard_map/while/body/eval_jaxpr/all_gather | solution.py:185
  58.3 42.9 %copy-start.20 = (f32[576]{0:T(1024)}, f32[576]{0:T(1024)S(1)}, u32[]{:S(2)}) copy-start(f32[576]{0:T(1024)S(1)} %fusion.171) | copy-start | bytes 6916 | tf_op jit(solution)/shard_map/while
  58.3 42.9 %copy-start.28 = (f32[576]{0:T(1024)}, f32[576]{0:T(1024)S(1)}, u32[]{:S(2)}) copy-start(f32[576]{0:T(1024)S(1)} %fusion.172) | copy-start | bytes 6916 | tf_op jit(solution)/shard_map/while
  58.4 42.9 %copy-start.26 = (f32[1024]{0:T(1024)}, f32[1024]{0:T(1024)S(1)}, u32[]{:S(2)}) copy-start(f32[1024]{0:T(1024)S(1)} %get-tuple-element.750) | copy-start | bytes 12292 | tf_op jit(solution)/shard_map/while
  58.4 42.9 %copy-start.3 = (bf16[2,576,1024]{2,1,0:T(8,128)(2,1)S(1)}, bf16[2,576,1024]{2,1,0:T(8,128)(2,1)}, u32[]{:S(2)}) copy-start(bf16[2,576,1024]{2,1,0:T(8,128)(2,1)} %get-tuple-element.915) | copy-start | bytes 7077892 | tf_op jit(solution)/shard_map/while
  107.4 23.4 %all-gather.18.cloned.1.call-start = ((), (), s32[]{:S(2)}) async-start(), calls=%async_computation.10 | async-start | bytes 3538944 | tf_op jit(solution)/shard_map/while/body/eval_jaxpr/all_gather | solution.py:184
  108.2 118.3 %all-gather.20.cloned.1.call-start = ((), (), s32[]{:S(2)}) async-start(), calls=%async_computation.11 | async-start | bytes 11894784 | tf_op jit(solution)/shard_map/while/body/eval_jaxpr/all_gather | solution.py:299
  108.7 186.7 %all-gather.22.cloned.1.call-start = ((), (), s32[]{:S(2)}) async-start(), calls=%async_computation.12 | async-start | bytes 5947392 | tf_op jit(solution)/shard_map/while/body/eval_jaxpr/all_gather | solution.py:307
  109.3 362.9 %reduce-scatter.12.cloned.1.call-start = ((), (), s32[]{:S(2)}) async-start(), calls=%async_computation.13 | async-start | bytes 3538944 | tf_op jit(solution)/shard_map/while/body/eval_jaxpr/reduce_scatter | solution.py:263
  200.8 123.8 %copy-start.30 = (f32[576]{0:T(1024)}, f32[576]{0:T(1024)S(1)}, u32[]{:S(2)}) copy-start(f32[576]{0:T(1024)S(1)} %fusion.175) | copy-start | bytes 6916 | tf_op jit(solution)/shard_map/while
  427.3 44.9 %reduce-scatter.14.cloned.1.call-start = ((), (), s32[]{:S(2)}) async-start(), calls=%async_computation.14 | async-start | bytes 3538944 | tf_op jit(solution)/shard_map/while/body/eval_jaxpr/reduce_scatter | solution.py:260
  506.0 85.1 %copy-start.10 = (bf16[1024,176]{0,1:T(8,128)(2,1)}, bf16[1024,176]{0,1:T(8,128)(2,1)S(1)}, u32[]{:S(2)}) copy-start(bf16[1024,176]{0,1:T(8,128)(2,1)S(1)} %get-tuple-element.921) | copy-start | bytes 1081348 | tf_op jit(solution)/shard_map/while
  506.0 85.1 %copy-start.14 = (bf16[88,1024]{1,0:T(8,128)(2,1)}, bf16[88,1024]{1,0:T(8,128)(2,1)S(1)}, u32[]{:S(2)}) copy-start(bf16[88,1024]{1,0:T(8,128)(2,1)S(1)} %get-tuple-element.922) | copy-start | bytes 540676 | tf_op jit(solution)/shard_map/while
  506.0 81.6 %all-gather.14.cloned.1.call-start = ((), (), s32[]{:S(2)}) async-start(), calls=%async_computation.8 | async-start | bytes 8650752 | tf_op jit(solution)/shard_map/while/body/eval_jaxpr/all_gather | solution.py:298
  506.8 100.2 %all-gather.16.cloned.1.call-start = ((), (), s32[]{:S(2)}) async-start(), calls=%async_computation.9 | async-start | bytes 3538944 | tf_op jit(solution)/shard_map/while/body/eval_jaxpr/all_gather | solution.py:185
  549.6 41.5 %copy-start.20 = (f32[576]{0:T(1024)}, f32[576]{0:T(1024)S(1)}, u32[]{:S(2)}) copy-start(f32[576]{0:T(1024)S(1)} %fusion.171) | copy-start | bytes 6916 | tf_op jit(solution)/shard_map/while
  549.6 41.5 %copy-start.28 = (f32[576]{0:T(1024)}, f32[576]{0:T(1024)S(1)}, u32[]{:S(2)}) copy-start(f32[576]{0:T(1024)S(1)} %fusion.172) | copy-start | bytes 6916 | tf_op jit(solution)/shard_map/while
  549.6 41.5 %copy-start.26 = (f32[1024]{0:T(1024)}, f32[1024]{0:T(1024)S(1)}, u32[]{:S(2)}) copy-start(f32[1024]{0:T(1024)S(1)} %get-tuple-element.750) | copy-start | bytes 12292 | tf_op jit(solution)/shard_map/while
  597.3 23.3 %all-gather.18.cloned.1.call-start = ((), (), s32[]{:S(2)}) async-start(), calls=%async_computation.10 | async-start | bytes 3538944 | tf_op jit(solution)/shard_map/while/body/eval_jaxpr/all_gather | solution.py:184
  597.9 118.5 %all-gather.20.cloned.1.call-start = ((), (), s32[]{:S(2)}) async-start(), calls=%async_computation.11 | async-start | bytes 11894784 | tf_op jit(solution)/shard_map/while/body/eval_jaxpr/all_gather | solution.py:299
  598.6 186.6 %all-gather.22.cloned.1.call-start = ((), (), s32[]{:S(2)}) async-start(), calls=%async_computation.12 | async-start | bytes 5947392 | tf_op jit(solution)/shard_map/while/body/eval_jaxpr/all_gather | solution.py:307
  599.2 371.6 %reduce-scatter.12.cloned.1.call-start = ((), (), s32[]{:S(2)}) async-start(), calls=%async_computation.13 | async-start | bytes 3538944 | tf_op jit(solution)/shard_map/while/body/eval_jaxpr/reduce_scatter | solution.py:263
  690.5 124.3 %copy-start.30 = (f32[576]{0:T(1024)}, f32[576]{0:T(1024)S(1)}, u32[]{:S(2)}) copy-start(f32[576]{0:T(1024)S(1)} %fusion.175) | copy-start | bytes 6916 | tf_op jit(solution)/shard_map/while
  917.4 53.4 %reduce-scatter.14.cloned.1.call-start = ((), (), s32[]{:S(2)}) async-start(), calls=%async_computation.14 | async-start | bytes 3538944 | tf_op jit(solution)/shard_map/while/body/eval_jaxpr/reduce_scatter | solution.py:260
  1011.6 167.5 %reduce-scatter.10.cloned.1.call-start = ((), (), s32[]{:S(2)}) async-start(), calls=%async_computation.7 | async-start | bytes 11894784 | tf_op jit(solution)/shard_map/reduce_scatter | solution.py:321
  1025.0 335.1 %reduce-scatter.6.cloned.1.call-start = ((), (), s32[]{:S(2)}) async-start(), calls=%async_computation.5 | async-start | bytes 17301504 | tf_op jit(solution)/shard_map/reduce_scatter | solution.py:319
  1043.1 567.0 %reduce-scatter.8.cloned.1.call-start = ((), (), s32[]{:S(2)}) async-start(), calls=%async_computation.6 | async-start | bytes 23789568 | tf_op jit(solution)/shard_map/reduce_scatter | solution.py:320
  1361.9 300.1 %copy-start.19 = (f32[1024,128]{1,0:T(8,128)S(1)}, f32[1024,128]{1,0:T(8,128)}, u32[]{:S(2)}) copy-start(f32[1024,128]{1,0:T(8,128)} %reduce-scatter.6.cloned.1.call-done) | copy-start | bytes 1572868
  1610.1 51.7 %copy-start.17 = (f32[1408,128]{1,0:T(8,128)S(1)}, f32[1408,128]{1,0:T(8,128)}, u32[]{:S(2)}) copy-start(f32[1408,128]{1,0:T(8,128)} %reduce-scatter.8.cloned.1.call-done) | copy-start | bytes 2162692
  (63 other events, 467.1 us)
Sparse Core Ops, SparseCore 0:
  16.8 80.9 all-gather.13
  107.5 9.5 all-gather.15
  118.7 12.1 all-gather.17
  134.1 92.3 all-gather.19
  229.8 65.6 all-gather.21
  427.5 8.8 reduce-scatter.11
  438.7 11.0 reduce-scatter.13
  510.3 77.2 all-gather.13
  597.4 9.5 all-gather.15
  608.4 12.1 all-gather.17
  624.0 92.3 all-gather.19
  719.6 65.5 all-gather.21
  917.5 8.8 reduce-scatter.11
  928.6 11.0 reduce-scatter.13
Sparse Core Ops, SparseCore 1:
  1025.0 154.0 reduce-scatter.9
  1181.2 178.8 reduce-scatter.5
  1362.3 247.8 reduce-scatter.7
where the time goes:
time: 1680 us
  waiting for transfers between devices  772 us (46%)
  matrix products  350 us (21%)
  local copies, waits for them, and re-layouts  247 us (15%)
  blocking collectives  170 us (10%)
  other arithmetic  110 us (7%)
  between operations  20.4 us (1%)
    reduce_scatter x1, waiting for transfers between devices, local(): lax.psum_scatter(flat_list[1], ('dp', 'fsdp'), scatter_dimension=0, tiled...  248 us
    reduce_scatter x1, waiting for transfers between devices, local(): lax.psum_scatter(flat_list[0], ('dp', 'fsdp'), scatter_dimension=0, tiled...  179 us
    all_gather x2, waiting for transfers between devices, micro_step(): lax.all_gather(narrow_low, ('dp', 'fsdp'), axis=0, tiled=True)  111 us
    while x2, blocking collectives  82.8 us
    dynamic_slice x96, local copies, waits for them, and re-layouts, forward(): lax.map(lambda pieces: pair_forward(pieces[0], pieces[1], pieces[2], same...  77.6 us
    all_gather x2, waiting for transfers between devices, micro_step(): lax.all_gather(attention_low, ('dp', 'fsdp'), axis=0, tiled=True)  77.3 us
    reduce_scatter x1, waiting for transfers between devices, local(): lax.psum_scatter(flat_list[2], ('dp', 'fsdp'), scatter_dimension=0, tiled...  67.6 us
    dot_general x6, matrix products, contract_rows(): lax.dot_general(left, right, (((0,), (0,)), ((), ())), preferred_element_...  66.5 us
  transfers between devices with their start and end apart: 17, of which 13 were waited for; matrix products, arithmetic and copies ran while one was open for 19% of the time, Pallas kernels for 0%

commit v1 on v0

--- a/solution.py
+++ b/solution.py
@@ -328,7 +328,7 @@
         + jnp.sum(reduced[2] * reduced[2])
         + jnp.sum(reduced[3] * reduced[3])
     )
-    grad_norm = jnp.sqrt(lax.psum(local_squares, ("dp", "fsdp")))
+    grad_norm = jnp.sqrt(lax.psum(lax.psum(local_squares, axis_name="fsdp"), axis_name="dp"))
     clip_factor = jnp.minimum(1.0, CLIP_LIMIT / (grad_norm + 1e-06))
     step_value = jnp.float32(STEP_VALUE)
     factors = (

time: 1680 us -> 1690 us (level)
    psum x1 -> x2, blocking collectives: 44.6 us -> 49.6 us  [the longest x1 44.5 us: local(): lax.psum(lax.psum(local_squares, axis_name='fsdp'), axis_name='dp')]
where the time goes in v1:
time: 1690 us; the launch traced here: 1680 us
  waiting for transfers between devices  772 us (46%)
  matrix products  350 us (21%)
  local copies, waits for them, and re-layouts  247 us (15%)
  blocking collectives  175 us (10%)
  other arithmetic  110 us (7%)
  between operations  20.4 us (1%)
    reduce_scatter x1, waiting for transfers between devices, local(): lax.psum_scatter(flat_list[1], ('dp', 'fsdp'), scatter_dimension=0, tiled...  248 us
    reduce_scatter x1, waiting for transfers between devices, local(): lax.psum_scatter(flat_list[0], ('dp', 'fsdp'), scatter_dimension=0, tiled...  179 us
    all_gather x2, waiting for transfers between devices, micro_step(): lax.all_gather(narrow_low, ('dp', 'fsdp'), axis=0, tiled=True)  111 us
    while x2, blocking collectives  82.8 us
    dynamic_slice x96, local copies, waits for them, and re-layouts, forward(): lax.map(lambda pieces: pair_forward(pieces[0], pieces[1], pieces[2], same...  77.6 us
    all_gather x2, waiting for transfers between devices, micro_step(): lax.all_gather(attention_low, ('dp', 'fsdp'), axis=0, tiled=True)  77.3 us
    reduce_scatter x1, waiting for transfers between devices, local(): lax.psum_scatter(flat_list[2], ('dp', 'fsdp'), scatter_dimension=0, tiled...  67.2 us
    dot_general x6, matrix products, contract_rows(): lax.dot_general(left, right, (((0,), (0,)), ((), ())), preferred_element_...  66.5 us
  transfers between devices with their start and end apart: 17, of which 13 were waited for; matrix products, arithmetic and copies ran while one was open for 19% of the time, Pallas kernels for 0%

profile of v1, /device:TPU:0, one launch (start us, length us, event | category | flops | bytes accessed | tf_op | source)
XLA Modules:
  0.0 1682.6 jit_solution(1974041498694560275)
XLA Ops:
  12.5 999.2 %while.73 = (s32[]{:T(128)}, f32[4096,1024]{1,0:T(8,128)}, f32[5632,1024]{1,0:T(8,128)}, f32[2816,1024]{1,0:T(8,128)}, f32[2048]{0:T(1024)}, /*index=5*/f32[2,57...) while((s32[]{:T(128)}, f32[4096,1024]{1,0:T(8,128)}, ...), condition=%wide.region_18.19_spmd.clone, body=%wide.region_0.18_spmd.clone.sunk | while | flops 45746876416 | bytes 740799360 | solution.py:314
  14.2 42.5 %all-reduce.4 = bf16[2048]{0:T(1024)(128)(2,1)S(1)} all-reduce(bf16[2048]{0:T(1024)(128)(2,1)S(1)} %dynamic-update-slice.3), channel_id=1, replica_groups=mesh['dp'=16,'fsdp'=2] {'dp','fsdp'}, use_global_device_ids=true, to_apply=%add | all-reduce | flops 2048 | bytes 8192 | tf_op jit(solution)/shard_map/while
  58.4 39.4 %all-gather.14.cloned.1.call-done = bf16[4096,1024]{1,0:T(8,128)(2,1)} async-done(((bf16[128,1024]{1,0:T(8,128)(2,1)}), bf16[4096,1024]{1,0:T(8,128)(2,1)}) %all-gather.14.cloned.1.call-update) | async-done | bytes 8388624 | tf_op jit(solution)/shard_map/while/body/eval_jaxpr/all_gather | solution.py:298
  120.1 10.7 all-gather.18.cloned.1.call-done
  136.4 59.3 %while.74 = (s32[]{:T(128)}, bf16[8,576,128]{1,2,0:T(8,128)(2,1)}, f32[8,2,576]{2,1,0:T(2,128)}, bf16[8,1152,128]{1,2,0:T(8,128)(2,1)S(1)}, bf16[8,576,128]{1,2,...) while((s32[]{:T(128)}, bf16[8,576,128]{1,2,0:T(8,128)(2,1)}, ...), condition=%wide.region_7.7_spmd.clone, body=%wide.region_4.6_spmd.clone.sunk | while | flops 349690752 | bytes 19968356 | solution.py:187
  200.8 25.8 %all-gather.20.cloned.1.call-done = bf16[1024,5632]{0,1:T(8,128)(2,1)} async-done(((bf16[1024,176]{0,1:T(8,128)(2,1)}), bf16[1024,5632]{0,1:T(8,128)(2,1)}) %all-gather.20.cloned.1.call-update) | async-done | bytes 11534352 | tf_op jit(solution)/shard_map/while/body/eval_jaxpr/all_gather | solution.py:299
  226.7 13.3 fusion.176
  239.9 55.7 %all-gather.22.cloned.1.call-done = bf16[2816,1024]{1,0:T(8,128)(2,1)} async-done(((bf16[88,1024]{1,0:T(8,128)(2,1)}), bf16[2816,1024]{1,0:T(8,128)(2,1)}) %all-gather.22.cloned.1.call-update) | async-done | bytes 5767184 | tf_op jit(solution)/shard_map/while/body/eval_jaxpr/all_gather | solution.py:307
  295.6 16.1 fusion.177
  311.7 13.0 multiply_reduce_fusion.12
  332.6 90.7 %while.75 = (s32[]{:T(128)}, bf16[8,576,128]{1,2,0:T(8,128)(2,1)}, bf16[8,1152,128]{1,2,0:T(8,128)(2,1)}, bf16[8,1152,128]{1,2,0:T(8,128)(2,1)}, bf16[8,1152,128...) while((s32[]{:T(128)}, bf16[8,576,128]{1,2,0:T(8,128)(2,1)}, ...), condition=%wide.region_12.12_spmd.clone, body=%wide.region_10.11_spmd.clone.sunk | while | flops 860625792 | bytes 46643592 | solution.py:247
  456.4 16.1 select_add_fusion.4
  492.5 10.9 bitcast_add_fusion.2
  508.0 40.3 %all-reduce.4 = bf16[2048]{0:T(1024)(128)(2,1)S(1)} all-reduce(bf16[2048]{0:T(1024)(128)(2,1)S(1)} %dynamic-update-slice.3), channel_id=1, replica_groups=mesh['dp'=16,'fsdp'=2] {'dp','fsdp'}, use_global_device_ids=true, to_apply=%add | all-reduce | flops 2048 | bytes 8192 | tf_op jit(solution)/shard_map/while
  549.9 38.0 %all-gather.14.cloned.1.call-done = bf16[4096,1024]{1,0:T(8,128)(2,1)} async-done(((bf16[128,1024]{1,0:T(8,128)(2,1)}), bf16[4096,1024]{1,0:T(8,128)(2,1)}) %all-gather.14.cloned.1.call-update) | async-done | bytes 8388624 | tf_op jit(solution)/shard_map/while/body/eval_jaxpr/all_gather | solution.py:298
  626.3 59.3 %while.74 = (s32[]{:T(128)}, bf16[8,576,128]{1,2,0:T(8,128)(2,1)}, f32[8,2,576]{2,1,0:T(2,128)}, bf16[8,1152,128]{1,2,0:T(8,128)(2,1)S(1)}, bf16[8,576,128]{1,2,...) while((s32[]{:T(128)}, bf16[8,576,128]{1,2,0:T(8,128)(2,1)}, ...), condition=%wide.region_7.7_spmd.clone, body=%wide.region_4.6_spmd.clone.sunk | while | flops 349690752 | bytes 19968356 | solution.py:187
  690.8 25.9 %all-gather.20.cloned.1.call-done = bf16[1024,5632]{0,1:T(8,128)(2,1)} async-done(((bf16[1024,176]{0,1:T(8,128)(2,1)}), bf16[1024,5632]{0,1:T(8,128)(2,1)}) %all-gather.20.cloned.1.call-update) | async-done | bytes 11534352 | tf_op jit(solution)/shard_map/while/body/eval_jaxpr/all_gather | solution.py:299
  716.7 13.3 fusion.176
  730.0 55.6 %all-gather.22.cloned.1.call-done = bf16[2816,1024]{1,0:T(8,128)(2,1)} async-done(((bf16[88,1024]{1,0:T(8,128)(2,1)}), bf16[2816,1024]{1,0:T(8,128)(2,1)}) %all-gather.22.cloned.1.call-update) | async-done | bytes 5767184 | tf_op jit(solution)/shard_map/while/body/eval_jaxpr/all_gather | solution.py:307
  785.6 16.4 fusion.177
  802.1 13.0 multiply_reduce_fusion.12
  823.0 90.6 %while.75 = (s32[]{:T(128)}, bf16[8,576,128]{1,2,0:T(8,128)(2,1)}, bf16[8,1152,128]{1,2,0:T(8,128)(2,1)}, bf16[8,1152,128]{1,2,0:T(8,128)(2,1)}, bf16[8,1152,128...) while((s32[]{:T(128)}, bf16[8,576,128]{1,2,0:T(8,128)(2,1)}, ...), condition=%wide.region_12.12_spmd.clone, body=%wide.region_10.11_spmd.clone.sunk | while | flops 860625792 | bytes 46643592 | solution.py:247
  949.3 22.0 %select_add_fusion.4 = f32[5632,1024]{1,0:T(8,128)} fusion(f32[5632,1024]{1,0:T(8,128)} %get-tuple-element.887, pred[]{:T(512)S(6)} %compare.3, bf16[576,2816]{1,0:T(8,128)(2,1)} %copy-done.44, bf16[576,2816]{1,0:T(8,128)(2,1)} %copy-done.43, f32[576,1024]{1,0:T(8,128)S(1)} %copy-done.6, f32[1024]{0:T(1024)S(1)} %get-tuple-element.758, ...), kind=kOutput, calls=%fused_computation.27.clone.1 | convolution fusion | flops 6670057472 | bytes 54991104 | tf_op jit(solution)/shard_map/while/body/eval_jaxpr/dot_general | solution.py:50
  991.3 14.0 bitcast_add_fusion.2
  1011.8 13.3 reshape.263
  1025.1 18.0 %reshape.261 = f32[32768,128]{1,0:T(8,128)} reshape(f32[4096,1024]{1,0:T(8,128)} %get-tuple-element.288) | data formatting | bytes 33554432 | tf_op jit(solution)/shard_map/reshape | solution.py:71
  1043.3 24.6 %reshape.262 = f32[45056,128]{1,0:T(8,128)} reshape(f32[5632,1024]{1,0:T(8,128)} %get-tuple-element.289) | data formatting | bytes 46137344 | tf_op jit(solution)/shard_map/reshape | solution.py:72
  1068.6 42.6 %all-reduce.2 = f32[2048]{0:T(1024)S(1)} all-reduce(f32[2048]{0:T(1024)S(1)} %copy-done.34), channel_id=9, replica_groups=mesh['dp'=16,'fsdp'=2] {'dp','fsdp'}, use_global_device_ids=true, to_apply=%region_25.26.clone | all-reduce | flops 2048 | bytes 16384
  1111.9 67.2 %reduce-scatter.10.cloned.1.call-done = f32[704,128]{1,0:T(8,128)} async-done(((f32[22528,128]{1,0:T(8,128)}), f32[704,128]{1,0:T(8,128)}) %reduce-scatter.10.cloned.1.call-update) | async-done | bytes 360464 | tf_op jit(solution)/shard_map/reduce_scatter | solution.py:321
  1180.7 179.3 %reduce-scatter.6.cloned.1.call-done = f32[1024,128]{1,0:T(8,128)} async-done(((f32[32768,128]{1,0:T(8,128)}), f32[1024,128]{1,0:T(8,128)}) %reduce-scatter.6.cloned.1.call-update) | async-done | bytes 524304 | tf_op jit(solution)/shard_map/reduce_scatter | solution.py:319
  1361.8 248.3 %reduce-scatter.8.cloned.1.call-done = f32[1408,128]{1,0:T(8,128)} async-done(((f32[45056,128]{1,0:T(8,128)}), f32[1408,128]{1,0:T(8,128)}) %reduce-scatter.8.cloned.1.call-update) | async-done | bytes 720912 | tf_op jit(solution)/shard_map/reduce_scatter | solution.py:320
  1619.8 44.5 %psum.15 = f32[]{:T(128)} all-reduce(f32[]{:T(128)} %psum.14), channel_id=1, replica_groups=mesh['dp'=16,'fsdp'=2] {'dp'}, use_global_device_ids=true, to_apply=%region_28.29 | all-reduce | flops 1 | bytes 8 | tf_op jit(solution)/shard_map/psum | solution.py:331
  (650 shorter events, 535.5 us)
Async XLA Ops:
  12.5 88.7 %copy-start.10 = (bf16[1024,176]{0,1:T(8,128)(2,1)}, bf16[1024,176]{0,1:T(8,128)(2,1)S(1)}, u32[]{:S(2)}) copy-start(bf16[1024,176]{0,1:T(8,128)(2,1)S(1)} %get-tuple-element.921) | copy-start | bytes 1081348 | tf_op jit(solution)/shard_map/while
  12.5 88.7 %copy-start.14 = (bf16[88,1024]{1,0:T(8,128)(2,1)}, bf16[88,1024]{1,0:T(8,128)(2,1)S(1)}, u32[]{:S(2)}) copy-start(bf16[88,1024]{1,0:T(8,128)(2,1)S(1)} %get-tuple-element.922) | copy-start | bytes 540676 | tf_op jit(solution)/shard_map/while
  12.5 85.2 %all-gather.14.cloned.1.call-start = ((), (), s32[]{:S(2)}) async-start(), calls=%async_computation.8 | async-start | bytes 8650752 | tf_op jit(solution)/shard_map/while/body/eval_jaxpr/all_gather | solution.py:298
  13.3 103.9 %all-gather.16.cloned.1.call-start = ((), (), s32[]{:S(2)}) async-start(), calls=%async_computation.9 | async-start | bytes 3538944 | tf_op jit(solution)/shard_map/while/body/eval_jaxpr/all_gather | solution.py:185
  58.3 42.9 %copy-start.20 = (f32[576]{0:T(1024)}, f32[576]{0:T(1024)S(1)}, u32[]{:S(2)}) copy-start(f32[576]{0:T(1024)S(1)} %fusion.171) | copy-start | bytes 6916 | tf_op jit(solution)/shard_map/while
  58.3 42.9 %copy-start.28 = (f32[576]{0:T(1024)}, f32[576]{0:T(1024)S(1)}, u32[]{:S(2)}) copy-start(f32[576]{0:T(1024)S(1)} %fusion.172) | copy-start | bytes 6916 | tf_op jit(solution)/shard_map/while
  58.4 42.9 %copy-start.26 = (f32[1024]{0:T(1024)}, f32[1024]{0:T(1024)S(1)}, u32[]{:S(2)}) copy-start(f32[1024]{0:T(1024)S(1)} %get-tuple-element.750) | copy-start | bytes 12292 | tf_op jit(solution)/shard_map/while
  58.4 42.9 %copy-start.3 = (bf16[2,576,1024]{2,1,0:T(8,128)(2,1)S(1)}, bf16[2,576,1024]{2,1,0:T(8,128)(2,1)}, u32[]{:S(2)}) copy-start(bf16[2,576,1024]{2,1,0:T(8,128)(2,1)} %get-tuple-element.915) | copy-start | bytes 7077892 | tf_op jit(solution)/shard_map/while
  107.4 23.4 %all-gather.18.cloned.1.call-start = ((), (), s32[]{:S(2)}) async-start(), calls=%async_computation.10 | async-start | bytes 3538944 | tf_op jit(solution)/shard_map/while/body/eval_jaxpr/all_gather | solution.py:184
  108.2 118.5 %all-gather.20.cloned.1.call-start = ((), (), s32[]{:S(2)}) async-start(), calls=%async_computation.11 | async-start | bytes 11894784 | tf_op jit(solution)/shard_map/while/body/eval_jaxpr/all_gather | solution.py:299
  108.7 186.9 %all-gather.22.cloned.1.call-start = ((), (), s32[]{:S(2)}) async-start(), calls=%async_computation.12 | async-start | bytes 5947392 | tf_op jit(solution)/shard_map/while/body/eval_jaxpr/all_gather | solution.py:307
  109.3 363.2 %reduce-scatter.12.cloned.1.call-start = ((), (), s32[]{:S(2)}) async-start(), calls=%async_computation.13 | async-start | bytes 3538944 | tf_op jit(solution)/shard_map/while/body/eval_jaxpr/reduce_scatter | solution.py:263
  200.8 124.0 %copy-start.30 = (f32[576]{0:T(1024)}, f32[576]{0:T(1024)S(1)}, u32[]{:S(2)}) copy-start(f32[576]{0:T(1024)S(1)} %fusion.175) | copy-start | bytes 6916 | tf_op jit(solution)/shard_map/while
  427.6 44.9 %reduce-scatter.14.cloned.1.call-start = ((), (), s32[]{:S(2)}) async-start(), calls=%async_computation.14 | async-start | bytes 3538944 | tf_op jit(solution)/shard_map/while/body/eval_jaxpr/reduce_scatter | solution.py:260
  506.3 85.1 %copy-start.10 = (bf16[1024,176]{0,1:T(8,128)(2,1)}, bf16[1024,176]{0,1:T(8,128)(2,1)S(1)}, u32[]{:S(2)}) copy-start(bf16[1024,176]{0,1:T(8,128)(2,1)S(1)} %get-tuple-element.921) | copy-start | bytes 1081348 | tf_op jit(solution)/shard_map/while
  506.3 85.1 %copy-start.14 = (bf16[88,1024]{1,0:T(8,128)(2,1)}, bf16[88,1024]{1,0:T(8,128)(2,1)S(1)}, u32[]{:S(2)}) copy-start(bf16[88,1024]{1,0:T(8,128)(2,1)S(1)} %get-tuple-element.922) | copy-start | bytes 540676 | tf_op jit(solution)/shard_map/while
  506.3 81.6 %all-gather.14.cloned.1.call-start = ((), (), s32[]{:S(2)}) async-start(), calls=%async_computation.8 | async-start | bytes 8650752 | tf_op jit(solution)/shard_map/while/body/eval_jaxpr/all_gather | solution.py:298
  507.0 100.2 %all-gather.16.cloned.1.call-start = ((), (), s32[]{:S(2)}) async-start(), calls=%async_computation.9 | async-start | bytes 3538944 | tf_op jit(solution)/shard_map/while/body/eval_jaxpr/all_gather | solution.py:185
  549.8 41.5 %copy-start.20 = (f32[576]{0:T(1024)}, f32[576]{0:T(1024)S(1)}, u32[]{:S(2)}) copy-start(f32[576]{0:T(1024)S(1)} %fusion.171) | copy-start | bytes 6916 | tf_op jit(solution)/shard_map/while
  549.9 41.5 %copy-start.28 = (f32[576]{0:T(1024)}, f32[576]{0:T(1024)S(1)}, u32[]{:S(2)}) copy-start(f32[576]{0:T(1024)S(1)} %fusion.172) | copy-start | bytes 6916 | tf_op jit(solution)/shard_map/while
  549.9 41.5 %copy-start.26 = (f32[1024]{0:T(1024)}, f32[1024]{0:T(1024)S(1)}, u32[]{:S(2)}) copy-start(f32[1024]{0:T(1024)S(1)} %get-tuple-element.750) | copy-start | bytes 12292 | tf_op jit(solution)/shard_map/while
  597.5 23.3 %all-gather.18.cloned.1.call-start = ((), (), s32[]{:S(2)}) async-start(), calls=%async_computation.10 | async-start | bytes 3538944 | tf_op jit(solution)/shard_map/while/body/eval_jaxpr/all_gather | solution.py:184
  598.1 118.6 %all-gather.20.cloned.1.call-start = ((), (), s32[]{:S(2)}) async-start(), calls=%async_computation.11 | async-start | bytes 11894784 | tf_op jit(solution)/shard_map/while/body/eval_jaxpr/all_gather | solution.py:299
  598.9 186.8 %all-gather.22.cloned.1.call-start = ((), (), s32[]{:S(2)}) async-start(), calls=%async_computation.12 | async-start | bytes 5947392 | tf_op jit(solution)/shard_map/while/body/eval_jaxpr/all_gather | solution.py:307
  599.4 371.9 %reduce-scatter.12.cloned.1.call-start = ((), (), s32[]{:S(2)}) async-start(), calls=%async_computation.13 | async-start | bytes 3538944 | tf_op jit(solution)/shard_map/while/body/eval_jaxpr/reduce_scatter | solution.py:263
  690.8 124.3 %copy-start.30 = (f32[576]{0:T(1024)}, f32[576]{0:T(1024)S(1)}, u32[]{:S(2)}) copy-start(f32[576]{0:T(1024)S(1)} %fusion.175) | copy-start | bytes 6916 | tf_op jit(solution)/shard_map/while
  917.9 53.4 %reduce-scatter.14.cloned.1.call-start = ((), (), s32[]{:S(2)}) async-start(), calls=%async_computation.14 | async-start | bytes 3538944 | tf_op jit(solution)/shard_map/while/body/eval_jaxpr/reduce_scatter | solution.py:260
  1011.7 167.3 %reduce-scatter.10.cloned.1.call-start = ((), (), s32[]{:S(2)}) async-start(), calls=%async_computation.7 | async-start | bytes 11894784 | tf_op jit(solution)/shard_map/reduce_scatter | solution.py:321
  1025.1 335.0 %reduce-scatter.6.cloned.1.call-start = ((), (), s32[]{:S(2)}) async-start(), calls=%async_computation.5 | async-start | bytes 17301504 | tf_op jit(solution)/shard_map/reduce_scatter | solution.py:319
  1043.2 566.9 %reduce-scatter.8.cloned.1.call-start = ((), (), s32[]{:S(2)}) async-start(), calls=%async_computation.6 | async-start | bytes 23789568 | tf_op jit(solution)/shard_map/reduce_scatter | solution.py:320
  1361.8 305.2 %copy-start.19 = (f32[1024,128]{1,0:T(8,128)S(1)}, f32[1024,128]{1,0:T(8,128)}, u32[]{:S(2)}) copy-start(f32[1024,128]{1,0:T(8,128)} %reduce-scatter.6.cloned.1.call-done) | copy-start | bytes 1572868
  1610.2 56.7 %copy-start.17 = (f32[1408,128]{1,0:T(8,128)S(1)}, f32[1408,128]{1,0:T(8,128)}, u32[]{:S(2)}) copy-start(f32[1408,128]{1,0:T(8,128)} %reduce-scatter.8.cloned.1.call-done) | copy-start | bytes 2162692
  (63 other events, 467.0 us)
Sparse Core Ops, SparseCore 0:
  16.8 80.9 all-gather.13
  107.5 9.5 all-gather.15
  118.7 12.1 all-gather.17
  134.1 92.5 all-gather.19
  229.9 65.6 all-gather.21
  427.7 8.8 reduce-scatter.11
  439.0 11.0 reduce-scatter.13
  510.6 77.2 all-gather.13
  597.6 9.5 all-gather.15
  608.6 12.1 all-gather.17
  624.2 92.4 all-gather.19
  720.0 65.5 all-gather.21
  918.0 8.8 reduce-scatter.11
  929.1 11.0 reduce-scatter.13
Sparse Core Ops, SparseCore 1:
  1025.2 153.8 reduce-scatter.9
  1181.2 178.8 reduce-scatter.5
  1362.2 247.9 reduce-scatter.7
